TPU v7x, 32 devices: a whole 2x2x4 slice. The times are simulated.
32 devices in a mesh: dp: 8 (over y, x, core), tensor: 4 (over z).
Axes of the slice: x: 2, y: 2, z: 4, core: 2. Of those that a mesh axis runs over, the one named last changes fastest.
Arguments:
- hidden_in: float32 [8192, 1536], P(('dp', 'tensor')), may hold values from -6 to 6
- cotangent: float32 [8192, 1536], P(('dp', 'tensor')), may hold values from -6 to 6
- seq_lengths: int32 [8, 4], P('dp'), may hold values from 1 to 512, 1024 in all within a row
- query_weight: bfloat16 [1536, 1536], P('dp', 'tensor'), may hold values from -0.15625 to 0.15625
- key_weight: bfloat16 [1536, 768], P('dp', 'tensor'), may hold values from -0.15625 to 0.15625
- value_weight: bfloat16 [1536, 768], P('dp', 'tensor'), may hold values from -0.15625 to 0.15625
- output_weight: bfloat16 [1536, 1536], P('tensor', 'dp'), may hold values from -1.25 to 1.25
- w_gate: bfloat16 [1536, 4096], P('dp', 'tensor'), may hold values from -0.15625 to 0.15625
- w_up: bfloat16 [1536, 4096], P('dp', 'tensor'), may hold values from -0.15625 to 0.15625
- w_down: bfloat16 [4096, 1536], P('tensor', 'dp'), may hold values from -0.09375 to 0.09375
- gain_attn: bfloat16 [1536], P('dp'), may hold values from 0.099609375 to 1.8984375
- gain_mlp: bfloat16 [1536], P('dp'), may hold values from 0.099609375 to 1.8984375
Outputs:
- block_out: float32 [8192, 1536], P(('dp', 'tensor'))
- grad_input: float32 [8192, 1536], P(('dp', 'tensor'))
- grad_query: float32 [1536, 1536], P('dp', 'tensor')
- grad_key: float32 [1536, 768], P('dp', 'tensor')
- grad_value: float32 [1536, 768], P('dp', 'tensor')
- grad_output: float32 [1536, 1536], P('tensor', 'dp')
- grad_gate: float32 [1536, 4096], P('dp', 'tensor')
- grad_upproj: float32 [1536, 4096], P('dp', 'tensor')
- grad_down: float32 [4096, 1536], P('tensor', 'dp')
- grad_attnorm: float32 [1536], P('dp')
- grad_mlpnorm: float32 [1536], P('dp')
Inputs may be any that keep to these rules, and one draw needn't show every extreme that they name: `seq_lengths`: each row's lengths sum to 1024, and the longest of each row is exactly 512.
All inputs are finite; a program needn't handle non-finite values.
Results may differ from a plain program's by a relative error of at most 0.02.
Values may be sent and summed in bfloat16 or wider, within the bound.
No kernel may reach another device: no remote copies, remote signals or barrier semaphores. Data moves between devices by JAX's collectives and lax.ppermute only.
A program may use at most 128 MiB of HBM per device.

v0:
```python
import math
import jax
import jax.numpy as jnp
from jax import lax
from jax.sharding import PartitionSpec as P

QUERY_HEADS = 16
KEY_VALUE_HEADS = 8
HEAD_SIZE = 96
EPS = 1e-05
ROPE_BASE = 100000.0


def product(formula, left_side, right_side):
    return jnp.einsum(formula, left_side, right_side, preferred_element_type=jnp.float32)


def matrix_multiply(left_side, right_side):
    return jnp.dot(left_side, right_side, preferred_element_type=jnp.float32)


def multiply_by_transpose(left_side, right_side):
    return lax.dot_general(
        left_side, right_side, (((1,), (1,)), ((), ())), preferred_element_type=jnp.float32
    )


def transposed_times(left_side, right_side):
    return lax.dot_general(
        left_side, right_side, (((0,), (0,)), ((), ())), preferred_element_type=jnp.float32
    )


def positions_of(lengths_row, length_all):
    seq_ends = jnp.cumsum(lengths_row)
    seq_starts = seq_ends - lengths_row
    token_index = jnp.arange(length_all, dtype=jnp.int32)
    segment = jnp.sum((token_index[:, None] >= seq_ends[None, :]).astype(jnp.int32), axis=1)
    chosen = segment[:, None] == jnp.arange(lengths_row.shape[0], dtype=jnp.int32)[None, :]
    offsets = jnp.sum(jnp.where(chosen, seq_starts[None, :], 0), axis=1)
    return (segment, token_index - offsets)


def rope_tables(position, head_width):
    half_width = head_width // 2
    frequency = jnp.exp(
        -(2.0 * jnp.arange(half_width, dtype=jnp.float32) / head_width)
        * jnp.log(jnp.float32(ROPE_BASE))
    )
    angles = position.astype(jnp.float32)[:, None] * frequency[None, :]
    return (jnp.cos(angles), jnp.sin(angles))


def rotate_fwd(value_tensor, cosine, sine):
    half_width = value_tensor.shape[-1] // 2
    front_half = value_tensor[..., :half_width]
    back_half = value_tensor[..., half_width:]
    return jnp.concatenate(
        [front_half * cosine - back_half * sine, back_half * cosine + front_half * sine], axis=-1
    )


def inverse_rotation(value_tensor, cosine, sine):
    half_width = value_tensor.shape[-1] // 2
    front_half = value_tensor[..., :half_width]
    back_half = value_tensor[..., half_width:]
    return jnp.concatenate(
        [front_half * cosine + back_half * sine, back_half * cosine - front_half * sine], axis=-1
    )


def norm_forward(value_tensor, gain_vector):
    inverse = lax.rsqrt(jnp.mean(value_tensor * value_tensor, axis=-1, keepdims=True) + EPS)
    unit_rows = value_tensor * inverse
    return (unit_rows, inverse, (unit_rows * gain_vector.astype(jnp.float32)).astype(jnp.bfloat16))


def norm_backward(grad_normed, unit_rows, inverse, gain_vector):
    scaled = grad_normed * gain_vector.astype(jnp.float32)
    grad_gain = jnp.sum(grad_normed * unit_rows, axis=0)
    grad_rows = inverse * (
        scaled - unit_rows * jnp.mean(scaled * unit_rows, axis=-1, keepdims=True)
    )
    return (grad_rows, grad_gain)


def block_scores(query_block, key_rows, segment_block, index_block, segment, factor):
    scores = product("qkgd,skd->kgqs", query_block, key_rows) * factor
    length_all = key_rows.shape[0]
    allowed = (segment_block[:, None] == segment[None, :]) & (
        jnp.arange(length_all, dtype=jnp.int32)[None, :] <= index_block[:, None]
    )
    return jnp.where(allowed[None, None], scores, -jnp.inf)


def attend(queries, key_rows, value_row_block, segment, block_rows):
    length_all, kv_heads, query_group_width, head_width = queries.shape
    blocks = length_all // block_rows
    factor = 1.0 / math.sqrt(head_width)
    token_index = jnp.arange(length_all, dtype=jnp.int32)

    def per_block(pieces):
        query_block, segment_block, index_block = pieces
        scores = block_scores(query_block, key_rows, segment_block, index_block, segment, factor)
        maximum = jnp.max(scores, axis=-1, keepdims=True)
        logsum = maximum + jnp.log(jnp.sum(jnp.exp(scores - maximum), axis=-1, keepdims=True))
        weights = jnp.exp(scores - logsum).astype(jnp.bfloat16)
        mixed = product("kgqs,skd->qkgd", weights, value_row_block).astype(jnp.bfloat16)
        return (mixed, logsum[..., 0])

    mixed, logsum = lax.map(
        per_block,
        (
            queries.reshape(blocks, block_rows, kv_heads, query_group_width, head_width),
            segment.reshape(blocks, block_rows),
            token_index.reshape(blocks, block_rows),
        ),
    )
    return (mixed.reshape(length_all, kv_heads, query_group_width, head_width), logsum)


def attend_back(
    queries, key_rows, value_row_block, mixed, mixed_gradient, logsum, segment, block_rows
):
    length_all, kv_heads, query_group_width, head_width = queries.shape
    blocks = length_all // block_rows
    factor = 1.0 / math.sqrt(head_width)
    token_index = jnp.arange(length_all, dtype=jnp.int32)

    def per_block(carry, pieces):
        grad_keys, grad_values = carry
        query_block, mixed_block, grad_block, logsum_block, segment_block, index_block = pieces
        scores = block_scores(query_block, key_rows, segment_block, index_block, segment, factor)
        probability = jnp.exp(scores - logsum_block[..., None])
        grad_values = grad_values + product(
            "kgqs,qkgd->skd", probability.astype(jnp.bfloat16), grad_block
        )
        grad_probs = product("qkgd,skd->kgqs", grad_block, value_row_block)
        row_delta = jnp.sum(
            grad_block.astype(jnp.float32) * mixed_block.astype(jnp.float32), axis=-1
        )
        row_delta = jnp.transpose(row_delta, (1, 2, 0))[..., None]
        grad_scores = (probability * (grad_probs - row_delta) * factor).astype(jnp.bfloat16)
        grad_query = product("kgqs,skd->qkgd", grad_scores, key_rows)
        grad_keys = grad_keys + product("kgqs,qkgd->skd", grad_scores, query_block)
        return ((grad_keys, grad_values), grad_query)

    empty_grad = jnp.zeros((length_all, kv_heads, head_width), jnp.float32)
    shape_blocks = (blocks, block_rows, kv_heads, query_group_width, head_width)
    (grad_keys, grad_values), grad_query = lax.scan(
        per_block,
        (empty_grad, empty_grad),
        (
            queries.reshape(shape_blocks),
            mixed.reshape(shape_blocks),
            mixed_gradient.reshape(shape_blocks),
            logsum,
            segment.reshape(blocks, block_rows),
            token_index.reshape(blocks, block_rows),
        ),
    )
    return (
        grad_query.reshape(length_all, kv_heads, query_group_width, head_width),
        grad_keys,
        grad_values,
    )


def local(
    hidden_in,
    cotangent,
    seq_lengths,
    query_weight,
    key_weight,
    value_weight,
    output_weight,
    w_gate,
    w_up,
    w_down,
    gain_attn,
    gain_mlp,
):
    query_group_width = QUERY_HEADS // KEY_VALUE_HEADS
    gathered = (
        lax.all_gather(query_weight, "dp", axis=0, tiled=True),
        lax.all_gather(key_weight, "dp", axis=0, tiled=True),
        lax.all_gather(value_weight, "dp", axis=0, tiled=True),
        lax.all_gather(output_weight, "dp", axis=1, tiled=True),
        lax.all_gather(w_gate, "dp", axis=0, tiled=True),
        lax.all_gather(w_up, "dp", axis=0, tiled=True),
        lax.all_gather(w_down, "dp", axis=1, tiled=True),
        lax.all_gather(gain_attn, "dp", axis=0, tiled=True),
        lax.all_gather(gain_mlp, "dp", axis=0, tiled=True),
    )
    (
        query_full,
        key_full,
        value_full,
        output_full,
        gate_full,
        up_full,
        down_full,
        gain_one,
        gain_two,
    ) = gathered
    kv_local = key_full.shape[1] // HEAD_SIZE
    unit_one, inverse_one, normed_rows_one = norm_forward(hidden_in, gain_one)
    first_normalized = lax.all_gather(normed_rows_one, "tensor", axis=0, tiled=True)
    tok_rows = first_normalized.shape[0]
    block_rows = min(512, tok_rows)
    segment, position = positions_of(seq_lengths[0], tok_rows)
    cosine, sine = rope_tables(position, HEAD_SIZE)
    cos_heads, sin_heads = (cosine[:, None, None, :], sine[:, None, None, :])
    cosine_key_table, sine_key_table = (cosine[:, None, :], sine[:, None, :])
    unrotated_queries = matrix_multiply(first_normalized, query_full).reshape(
        tok_rows, kv_local, query_group_width, HEAD_SIZE
    )
    unrotated_keys = matrix_multiply(first_normalized, key_full).reshape(
        tok_rows, kv_local, HEAD_SIZE
    )
    value_row_block = (
        matrix_multiply(first_normalized, value_full)
        .astype(jnp.bfloat16)
        .reshape(tok_rows, kv_local, HEAD_SIZE)
    )
    query_rot = rotate_fwd(unrotated_queries, cos_heads, sin_heads).astype(jnp.bfloat16)
    key_rot = rotate_fwd(unrotated_keys, cosine_key_table, sine_key_table).astype(jnp.bfloat16)
    query_rot, key_rot, value_row_block = (query_rot, key_rot, value_row_block)
    mixed, logsum = attend(query_rot, key_rot, value_row_block, segment, block_rows)
    mixed_flat = mixed.reshape(tok_rows, -1)
    residual = hidden_in + lax.psum_scatter(
        matrix_multiply(mixed_flat, output_full), "tensor", scatter_dimension=0, tiled=True
    )
    unit_two, inverse_two, normed_rows_two = norm_forward(residual, gain_two)
    normed_two = lax.all_gather(normed_rows_two, "tensor", axis=0, tiled=True)
    gate_rows = matrix_multiply(normed_two, gate_full)
    up_rows = matrix_multiply(normed_two, up_full)
    sigmoid_gate = jax.nn.sigmoid(gate_rows)
    silu_gate = gate_rows * sigmoid_gate
    project_hidden_act = (silu_gate * up_rows).astype(jnp.bfloat16)
    gate_rows, up_rows, sigmoid_gate, silu_gate, hidden_act = (
        gate_rows,
        up_rows,
        sigmoid_gate,
        silu_gate,
        project_hidden_act,
    )
    block_out = residual + lax.psum_scatter(
        matrix_multiply(hidden_act, down_full).astype(jnp.bfloat16),
        "tensor",
        scatter_dimension=0,
        tiled=True,
    ).astype(jnp.float32)
    gathered = (
        lax.all_gather(query_weight, "dp", axis=0, tiled=True),
        lax.all_gather(key_weight, "dp", axis=0, tiled=True),
        lax.all_gather(value_weight, "dp", axis=0, tiled=True),
        lax.all_gather(output_weight, "dp", axis=1, tiled=True),
        lax.all_gather(w_gate, "dp", axis=0, tiled=True),
        lax.all_gather(w_up, "dp", axis=0, tiled=True),
        lax.all_gather(w_down, "dp", axis=1, tiled=True),
        lax.all_gather(gain_attn, "dp", axis=0, tiled=True),
        lax.all_gather(gain_mlp, "dp", axis=0, tiled=True),
    )
    (
        query_full,
        key_full,
        value_full,
        output_full,
        gate_full,
        up_full,
        down_full,
        gain_one,
        gain_two,
    ) = gathered
    cot_low = lax.all_gather(cotangent.astype(jnp.bfloat16), "tensor", axis=0, tiled=True)
    grad_act = multiply_by_transpose(cot_low, down_full)
    grad_down = transposed_times(hidden_act, cot_low)
    grad_gate_rows = (
        grad_act * up_rows * sigmoid_gate * (1.0 + gate_rows * (1.0 - sigmoid_gate))
    ).astype(jnp.bfloat16)
    grad_up_rows = (grad_act * silu_gate).astype(jnp.bfloat16)
    grad_gate = transposed_times(normed_two, grad_gate_rows)
    grad_upproj = transposed_times(normed_two, grad_up_rows)
    grad_normed_two = lax.psum_scatter(
        (
            multiply_by_transpose(grad_gate_rows, gate_full)
            + multiply_by_transpose(grad_up_rows, up_full)
        ).astype(jnp.bfloat16),
        "tensor",
        scatter_dimension=0,
        tiled=True,
    ).astype(jnp.float32)
    grad_middle, grad_gain_two = norm_backward(grad_normed_two, unit_two, inverse_two, gain_two)
    grad_resid = cotangent + grad_middle
    narrow_gradient = lax.all_gather(grad_resid.astype(jnp.bfloat16), "tensor", axis=0, tiled=True)
    grad_output = transposed_times(mixed_flat, narrow_gradient)
    mixed_gradient = (
        multiply_by_transpose(narrow_gradient, output_full)
        .astype(jnp.bfloat16)
        .reshape(tok_rows, kv_local, query_group_width, HEAD_SIZE)
    )
    grad_qrot, rotated_key_gradient, gradient_values_list = attend_back(
        query_rot, key_rot, value_row_block, mixed, mixed_gradient, logsum, segment, block_rows
    )
    grad_q = (
        inverse_rotation(grad_qrot, cos_heads, sin_heads).astype(jnp.bfloat16).reshape(tok_rows, -1)
    )
    key_gradient = (
        inverse_rotation(rotated_key_gradient, cosine_key_table, sine_key_table)
        .astype(jnp.bfloat16)
        .reshape(tok_rows, -1)
    )
    value_gradient = gradient_values_list.astype(jnp.bfloat16).reshape(tok_rows, -1)
    grad_query = transposed_times(first_normalized, grad_q)
    grad_key = transposed_times(first_normalized, key_gradient)
    grad_value = transposed_times(first_normalized, value_gradient)
    grad_normed_one = lax.psum_scatter(
        (
            multiply_by_transpose(grad_q, query_full)
            + multiply_by_transpose(key_gradient, key_full)
            + multiply_by_transpose(value_gradient, value_full)
        ).astype(jnp.bfloat16),
        "tensor",
        scatter_dimension=0,
        tiled=True,
    ).astype(jnp.float32)
    grad_first, grad_gain_one = norm_backward(grad_normed_one, unit_one, inverse_one, gain_one)
    grad_input = grad_resid + grad_first
    summed = (
        lax.psum_scatter(
            grad_query.astype(jnp.bfloat16), "dp", scatter_dimension=0, tiled=True
        ).astype(jnp.float32),
        lax.psum_scatter(
            grad_key.astype(jnp.bfloat16), "dp", scatter_dimension=0, tiled=True
        ).astype(jnp.float32),
        lax.psum_scatter(
            grad_value.astype(jnp.bfloat16), "dp", scatter_dimension=0, tiled=True
        ).astype(jnp.float32),
        lax.psum_scatter(
            grad_output.astype(jnp.bfloat16), "dp", scatter_dimension=1, tiled=True
        ).astype(jnp.float32),
        lax.psum_scatter(
            grad_gate.astype(jnp.bfloat16), "dp", scatter_dimension=0, tiled=True
        ).astype(jnp.float32),
        lax.psum_scatter(
            grad_upproj.astype(jnp.bfloat16), "dp", scatter_dimension=0, tiled=True
        ).astype(jnp.float32),
        lax.psum_scatter(
            grad_down.astype(jnp.bfloat16), "dp", scatter_dimension=1, tiled=True
        ).astype(jnp.float32),
        lax.psum_scatter(
            grad_gain_one.astype(jnp.bfloat16), "dp", scatter_dimension=0, tiled=True
        ).astype(jnp.float32),
        lax.psum_scatter(
            grad_gain_two.astype(jnp.bfloat16), "dp", scatter_dimension=0, tiled=True
        ).astype(jnp.float32),
    )
    output_grad = summed[3]
    gain_totals = lax.psum((summed[7], summed[8]), "tensor")
    return (
        block_out,
        grad_input,
        summed[0],
        summed[1],
        summed[2],
        output_grad,
        summed[4],
        summed[5],
        summed[6],
        gain_totals[0],
        gain_totals[1],
    )


def solution(mesh):
    in_specs = (
        P(("dp", "tensor"), None),
        P(("dp", "tensor"), None),
        P("dp", None),
        P("dp", "tensor"),
        P("dp", "tensor"),
        P("dp", "tensor"),
        P("tensor", "dp"),
        P("dp", "tensor"),
        P("dp", "tensor"),
        P("tensor", "dp"),
        P("dp"),
        P("dp"),
    )
    out_specs = (
        P(("dp", "tensor"), None),
        P(("dp", "tensor"), None),
        P("dp", "tensor"),
        P("dp", "tensor"),
        P("dp", "tensor"),
        P("tensor", "dp"),
        P("dp", "tensor"),
        P("dp", "tensor"),
        P("tensor", "dp"),
        P("dp"),
        P("dp"),
    )
    return jax.shard_map(local, mesh=mesh, in_specs=in_specs, out_specs=out_specs, check_vma=False)
```

profile of v0, /device:TPU:0, one launch (start us, length us, event | category | flops | bytes accessed | tf_op | source)
XLA Modules:
  0.0 1093.3 jit_solution(17131380025793593165)
XLA Ops:
  12.6 16.0 %all-reduce.6 = (bf16[1536]{0:T(1024)(128)(2,1)S(1)}, bf16[1536]{0:T(1024)(128)(2,1)}) all-reduce(bf16[1536]{0:T(1024)(128)(2,1)S(1)} %dynamic-update-slice, bf16[1536]{0:T(1024)(128)(2,1)S(1)} %dynamic-update-slice.1), channel_id=1, replica_groups=mesh['dp'=8,'tensor'=4] {'dp'}, use_global_device_ids=true, to_apply=%add | all-reduce | flops 3072 | bytes 12288
  56.3 37.9 %all-gather.10.cloned.1.call-done = bf16[1024,1536]{1,0:T(8,128)(2,1)} async-done(((bf16[256,1536]{1,0:T(8,128)(2,1)}), bf16[1024,1536]{1,0:T(8,128)(2,1)}) %all-gather.10.cloned.1.call-update) | async-done | bytes 3145744 | tf_op jit(solution)/shard_map/all_gather | solution.py:208
  98.4 20.2 %all-gather.12.cloned.1.call-done = bf16[1536,384]{1,0:T(8,128)(2,1)} async-done(((bf16[192,384]{1,0:T(8,128)(2,1)}), bf16[1536,384]{1,0:T(8,128)(2,1)}) %all-gather.12.cloned.1.call-update) | async-done | bytes 1179664 | tf_op jit(solution)/shard_map/all_gather | solution.py:185
  130.9 22.1 %while.27 = (s32[]{:T(128)}, bf16[2,512,2,2,96]{1,4,3,2,0:T(8,128)(2,1)}, f32[2,2,2,512]{3,2,1,0:T(2,128)}, s32[2,512]{1,0:T(2,128)}, s32[1024]{0:T(1024)S(1)}, ...) while((s32[]{:T(128)}, ...), condition=%wide.region_7.8_spmd, body=%wide.region_4.7_spmd.sunk | while | flops 830142464 | bytes 28917884 | solution.py:111
  161.9 110.3 %reduce-scatter.12.cloned.1.call-done = f32[256,1536]{1,0:T(8,128)} async-done(((f32[1024,1536]{1,0:T(8,128)}), f32[256,1536]{1,0:T(8,128)}) %reduce-scatter.12.cloned.1.call-update) | async-done | bytes 1572880 | tf_op jit(solution)/shard_map/reduce_scatter | solution.py:231
  279.2 27.5 %all-gather.20.cloned.1.call-done = bf16[1536,1024]{1,0:T(8,128)(2,1)} async-done(((bf16[192,1024]{1,0:T(8,128)(2,1)}), bf16[1536,1024]{1,0:T(8,128)(2,1)}) %all-gather.20.cloned.1.call-update) | async-done | bytes 3145744 | tf_op jit(solution)/shard_map/all_gather | solution.py:190
  306.6 65.5 %all-gather.16.cloned.1.call-done = bf16[1024,1536]{1,0:T(8,128)(2,1)} async-done(((bf16[256,1536]{1,0:T(8,128)(2,1)}), bf16[1024,1536]{1,0:T(8,128)(2,1)}) %all-gather.16.cloned.1.call-update) | async-done | bytes 3145744 | tf_op jit(solution)/shard_map/all_gather | solution.py:235
  380.4 24.5 %all-gather.18.cloned.1.call-done = bf16[1536,1024]{1,0:T(8,128)(2,1)} async-done(((bf16[192,1024]{1,0:T(8,128)(2,1)}), bf16[1536,1024]{1,0:T(8,128)(2,1)}) %all-gather.18.cloned.1.call-update) | async-done | bytes 3145744 | tf_op jit(solution)/shard_map/all_gather | solution.py:189
  413.1 57.4 %all-gather.24.cloned.1.call-done = bf16[1024,1536]{1,0:T(8,128)(2,1)} async-done(((bf16[256,1536]{1,0:T(8,128)(2,1)}), bf16[1024,1536]{1,0:T(8,128)(2,1)}) %all-gather.24.cloned.1.call-update) | async-done | bytes 3145744 | tf_op jit(solution)/shard_map/all_gather | solution.py:276
  470.5 32.7 %all-gather.22.cloned.1.call-done = bf16[1024,1536]{0,1:T(8,128)(2,1)} async-done(((bf16[1024,192]{0,1:T(8,128)(2,1)}), bf16[1024,1536]{0,1:T(8,128)(2,1)}) %all-gather.22.cloned.1.call-update) | async-done | bytes 3145744 | tf_op jit(solution)/shard_map/all_gather | solution.py:191
  523.5 60.5 %reduce-scatter.16.cloned.1.call-done = bf16[256,1536]{1,0:T(8,128)(2,1)} async-done(((bf16[1024,1536]{1,0:T(8,128)(2,1)}), bf16[256,1536]{1,0:T(8,128)(2,1)}) %reduce-scatter.16.cloned.1.call-update) | async-done | bytes 786448 | tf_op jit(solution)/shard_map/reduce_scatter | solution.py:285
  613.0 39.9 %all-gather.26.cloned.1.call-done = bf16[1024,1536]{1,0:T(8,128)(2,1)} async-done(((bf16[256,1536]{1,0:T(8,128)(2,1)}), bf16[1024,1536]{1,0:T(8,128)(2,1)}) %all-gather.26.cloned.1.call-update) | async-done | bytes 3145744 | tf_op jit(solution)/shard_map/all_gather | solution.py:296
  664.5 68.3 %while.28 = (s32[]{:T(128)}, f32[1024,2,96]{0,2,1:T(8,128)}, f32[1024,2,96]{0,2,1:T(8,128)}, f32[2,512,2,2,96]{1,0,4,3,2:T(2,128)}, bf16[2,512,2,2,96]{1,4,3,2,0...) while((s32[]{:T(128)}, f32[1024,2,96]{0,2,1:T(8,128)}, ...), condition=%wide.region_15.16_spmd.clone, body=%wide.region_13.15_spmd.clone.sunk | while | flops 2039478272 | bytes 50004156 | solution.py:150
  682.9 15.0 %dynamic_update_slice.20 = f32[2,512,2,2,96]{1,0,4,3,2:T(2,128)} dynamic-update-slice(f32[2,512,2,2,96]{1,0,4,3,2:T(2,128)} %get-tuple-element.535, f32[1,512,2,2,96]{1,0,4,3,2:T(1,128)S(1)} %copy.60, s32[]{:T(128)S(6)} %copy.79, s32[]{:T(128)} %constant.62.clone.1..sunk, s32[]{:T(128)} %constant.62.clone.1..sunk, s32[]{:T(128)} %constant.62.clone.1..sunk, s32[]{:T(128)} %constant.62.clone.1..sunk) | dynamic-update-slice | bytes 1572868 | tf_op jit(solution)/shard_map/while/body/jit(dynamic_update_index_in_dim)/dynamic_update_slice | solution.py:150
  717.8 15.0 %dynamic_update_slice.20 = f32[2,512,2,2,96]{1,0,4,3,2:T(2,128)} dynamic-update-slice(f32[2,512,2,2,96]{1,0,4,3,2:T(2,128)} %get-tuple-element.535, f32[1,512,2,2,96]{1,0,4,3,2:T(1,128)S(1)} %copy.60, s32[]{:T(128)S(6)} %copy.79, s32[]{:T(128)} %constant.62.clone.1..sunk, s32[]{:T(128)} %constant.62.clone.1..sunk, s32[]{:T(128)} %constant.62.clone.1..sunk, s32[]{:T(128)} %constant.62.clone.1..sunk) | dynamic-update-slice | bytes 1572868 | tf_op jit(solution)/shard_map/while/body/jit(dynamic_update_index_in_dim)/dynamic_update_slice | solution.py:150
  776.9 22.8 %reduce-scatter.28.cloned.1.call-done = bf16[192,1024]{1,0:T(8,128)(2,1)} async-done(((bf16[1536,1024]{1,0:T(8,128)(2,1)}), bf16[192,1024]{1,0:T(8,128)(2,1)}) %reduce-scatter.28.cloned.1.call-update) | async-done | bytes 393232 | tf_op jit(solution)/shard_map/reduce_scatter | solution.py:343
  801.6 36.0 %reduce-scatter.24.cloned.1.call-done = bf16[192,192]{1,0:T(8,128)(2,1)} async-done(((bf16[1536,192]{1,0:T(8,128)(2,1)}), bf16[192,192]{1,0:T(8,128)(2,1)}) %reduce-scatter.24.cloned.1.call-update) | async-done | bytes 73744 | tf_op jit(solution)/shard_map/reduce_scatter | solution.py:337
  839.2 36.4 %reduce-scatter.22.cloned.1.call-done = bf16[192,192]{1,0:T(8,128)(2,1)} async-done(((bf16[1536,192]{1,0:T(8,128)(2,1)}), bf16[192,192]{1,0:T(8,128)(2,1)}) %reduce-scatter.22.cloned.1.call-update) | async-done | bytes 73744 | tf_op jit(solution)/shard_map/reduce_scatter | solution.py:334
  877.2 38.8 %reduce-scatter.26.cloned.1.call-done = bf16[384,192]{0,1:T(8,128)(2,1)} async-done(((bf16[384,1536]{0,1:T(8,128)(2,1)}), bf16[384,192]{0,1:T(8,128)(2,1)}) %reduce-scatter.26.cloned.1.call-update) | async-done | bytes 147472 | tf_op jit(solution)/shard_map/reduce_scatter | solution.py:340
  917.6 38.7 %reduce-scatter.20.cloned.1.call-done = bf16[192,384]{1,0:T(8,128)(2,1)} async-done(((bf16[1536,384]{1,0:T(8,128)(2,1)}), bf16[192,384]{1,0:T(8,128)(2,1)}) %reduce-scatter.20.cloned.1.call-update) | async-done | bytes 147472 | tf_op jit(solution)/shard_map/reduce_scatter | solution.py:331
  958.0 61.1 %reduce-scatter.18.cloned.1.call-done = bf16[256,1536]{1,0:T(8,128)(2,1)} async-done(((bf16[1024,1536]{1,0:T(8,128)(2,1)}), bf16[256,1536]{1,0:T(8,128)(2,1)}) %reduce-scatter.18.cloned.1.call-update) | async-done | bytes 786448 | tf_op jit(solution)/shard_map/reduce_scatter | solution.py:318
  1020.8 13.5 %all-reduce.5 = (bf16[1536]{0:T(1024)(128)(2,1)S(1)}, bf16[1536]{0:T(1024)(128)(2,1)S(1)}) all-reduce(bf16[1536]{0:T(1024)(128)(2,1)S(1)} %get-tuple-element.256, bf16[1536]{0:T(1024)(128)(2,1)S(1)} %copy-done.32), channel_id=13, replica_groups=mesh['dp'=8,'tensor'=4] {'dp'}, use_global_device_ids=true, to_apply=%region_26.27.clone | all-reduce | flops 3072 | bytes 12288
  1034.4 12.1 %all-reduce.4 = (f32[192]{0:T(256)}, f32[192]{0:T(256)}) all-reduce(f32[192]{0:T(256)S(1)} %get-tuple-element.336, f32[192]{0:T(256)S(1)} %get-tuple-element.335), channel_id=1, replica_groups=mesh['dp'=8,'tensor'=4] {'tensor'}, use_global_device_ids=true, to_apply=%region_27.28 | all-reduce | flops 384 | bytes 3072 | tf_op jit(solution)/shard_map/psum | solution.py:360
  1046.5 35.3 %reduce-scatter.14.cloned.1.call-done = bf16[256,1536]{1,0:T(8,128)(2,1)} async-done(((bf16[1024,1536]{1,0:T(8,128)(2,1)}), bf16[256,1536]{1,0:T(8,128)(2,1)}) %reduce-scatter.14.cloned.1.call-update) | async-done | bytes 786448 | tf_op jit(solution)/shard_map/reduce_scatter | solution.py:248
  (239 shorter events, 259.5 us)
Async XLA Ops:
  7.2 87.0 %all-gather.10.cloned.1.call-start = ((), (), s32[]{:S(2)}) async-start(), calls=%async_computation.11 | async-start | bytes 3932160 | tf_op jit(solution)/shard_map/all_gather | solution.py:208
  31.2 87.4 %all-gather.12.cloned.1.call-start = ((), (), s32[]{:S(2)}) async-start(), calls=%async_computation.12 | async-start | bytes 1327104 | tf_op jit(solution)/shard_map/all_gather | solution.py:185
  31.9 123.2 %all-gather.14.cloned.1.call-start = ((), (), s32[]{:S(2)}) async-start(), calls=%async_computation.13 | async-start | bytes 1327104 | tf_op jit(solution)/shard_map/all_gather | solution.py:188
  32.7 239.5 %reduce-scatter.12.cloned.1.call-start = ((), (), s32[]{:S(2)}) async-start(), calls=%async_computation.14 | async-start | bytes 7864320 | tf_op jit(solution)/shard_map/reduce_scatter | solution.py:231
  161.2 145.4 %all-gather.20.cloned.1.call-start = ((), (), s32[]{:S(2)}) async-start(), calls=%async_computation.17 | async-start | bytes 3538944 | tf_op jit(solution)/shard_map/all_gather | solution.py:190
  161.8 210.3 %all-gather.16.cloned.1.call-start = ((), (), s32[]{:S(2)}) async-start(), calls=%async_computation.15 | async-start | bytes 3932160 | tf_op jit(solution)/shard_map/all_gather | solution.py:235
  276.1 128.8 %all-gather.18.cloned.1.call-start = ((), (), s32[]{:S(2)}) async-start(), calls=%async_computation.16 | async-start | bytes 3538944 | tf_op jit(solution)/shard_map/all_gather | solution.py:189
  276.8 193.6 %all-gather.24.cloned.1.call-start = ((), (), s32[]{:S(2)}) async-start(), calls=%async_computation.20 | async-start | bytes 3932160 | tf_op jit(solution)/shard_map/all_gather | solution.py:276
  277.9 225.3 %all-gather.22.cloned.1.call-start = ((), (), s32[]{:S(2)}) async-start(), calls=%async_computation.18 | async-start | bytes 3538944 | tf_op jit(solution)/shard_map/all_gather | solution.py:191
  278.6 305.4 %reduce-scatter.16.cloned.1.call-start = ((), (), s32[]{:S(2)}) async-start(), calls=%async_computation.21 | async-start | bytes 3932160 | tf_op jit(solution)/shard_map/reduce_scatter | solution.py:285
  523.4 129.4 %all-gather.26.cloned.1.call-start = ((), (), s32[]{:S(2)}) async-start(), calls=%async_computation.22 | async-start | bytes 3932160 | tf_op jit(solution)/shard_map/all_gather | solution.py:296
  589.4 183.5 %reduce-scatter.32.cloned.1.call-start = ((), (), s32[]{:S(2)}) async-start(), calls=%async_computation.30 | async-start | bytes 3538944 | tf_op jit(solution)/shard_map/reduce_scatter | solution.py:349
  597.1 177.8 %reduce-scatter.30.cloned.1.call-start = ((), (), s32[]{:S(2)}) async-start(), calls=%async_computation.29 | async-start | bytes 3538944 | tf_op jit(solution)/shard_map/reduce_scatter | solution.py:346
  605.1 194.5 %reduce-scatter.28.cloned.1.call-start = ((), (), s32[]{:S(2)}) async-start(), calls=%async_computation.28 | async-start | bytes 3538944 | tf_op jit(solution)/shard_map/reduce_scatter | solution.py:343
  612.9 224.7 %reduce-scatter.24.cloned.1.call-start = ((), (), s32[]{:S(2)}) async-start(), calls=%async_computation.26 | async-start | bytes 884736 | tf_op jit(solution)/shard_map/reduce_scatter | solution.py:337
  738.8 136.9 %reduce-scatter.22.cloned.1.call-start = ((), (), s32[]{:S(2)}) async-start(), calls=%async_computation.25 | async-start | bytes 884736 | tf_op jit(solution)/shard_map/reduce_scatter | solution.py:334
  745.5 170.5 %reduce-scatter.26.cloned.1.call-start = ((), (), s32[]{:S(2)}) async-start(), calls=%async_computation.27 | async-start | bytes 1327104 | tf_op jit(solution)/shard_map/reduce_scatter | solution.py:340
  750.3 206.0 %reduce-scatter.20.cloned.1.call-start = ((), (), s32[]{:S(2)}) async-start(), calls=%async_computation.24 | async-start | bytes 1327104 | tf_op jit(solution)/shard_map/reduce_scatter | solution.py:331
  757.8 261.3 %reduce-scatter.18.cloned.1.call-start = ((), (), s32[]{:S(2)}) async-start(), calls=%async_computation.23 | async-start | bytes 3932160 | tf_op jit(solution)/shard_map/reduce_scatter | solution.py:318
  763.9 317.9 %reduce-scatter.14.cloned.1.call-start = ((), (), s32[]{:S(2)}) async-start(), calls=%async_computation.19 | async-start | bytes 3932160 | tf_op jit(solution)/shard_map/reduce_scatter | solution.py:248
  772.1 246.9 %copy-start.1 = (f32[256,1536]{1,0:T(8,128)S(1)}, f32[256,1536]{1,0:T(8,128)}, u32[]{:S(2)}) copy-start(f32[256,1536]{1,0:T(8,128)} %param.16) | copy-start | bytes 4718596
  772.1 246.9 %copy-start.25 = (f32[1536]{0:T(1024)S(1)}, f32[1536]{0:T(1024)}, u32[]{:S(2)}) copy-start(f32[1536]{0:T(1024)} %copy-done.24) | copy-start | bytes 18436
  774.9 306.9 %copy-start.29 = (f32[256]{0:T(256)S(1)}, f32[256]{0:T(256)}, u32[]{:S(2)}) copy-start(f32[256]{0:T(256)} %copy-done.28) | copy-start | bytes 3076
  774.9 306.9 %copy-start.34 = (f32[256]{0:T(256)S(1)}, f32[256]{0:T(256)}, u32[]{:S(2)}) copy-start(f32[256]{0:T(256)} %copy-done.33) | copy-start | bytes 3076
  (37 other events, 1182.6 us)
Sparse Core Ops, SparseCore 0:
  31.3 62.7 all-gather.9
  96.0 22.5 all-gather.11
  120.5 23.9 all-gather.13
  161.4 110.7 reduce-scatter.11
  273.9 32.6 all-gather.19
  308.6 63.4 all-gather.15
  374.0 30.8 all-gather.17
  407.0 63.4 all-gather.23
  472.4 30.8 all-gather.21
  523.6 60.3 reduce-scatter.15
  589.5 63.3 all-gather.25
  656.1 44.6 reduce-scatter.31
  704.2 46.0 reduce-scatter.29
  753.6 46.0 reduce-scatter.27
  802.7 34.9 reduce-scatter.23
  840.6 34.9 reduce-scatter.21
  879.3 36.6 reduce-scatter.25
  919.6 36.6 reduce-scatter.19
  958.6 60.3 reduce-scatter.17
  1021.2 60.5 reduce-scatter.13
where the time goes:
time: 1100 us; the launch traced here: 1090 us
  waiting for transfers between devices  749 us (68%)
  matrix products  152 us (14%)
  blocking collectives  63.4 us (6%)
  local copies, waits for them, and re-layouts  60.7 us (6%)
  other arithmetic  49.9 us (5%)
  between operations  16.5 us (2%)
    reduce_scatter x1, waiting for transfers between devices, local(): lax.psum_scatter(matrix_multiply(mixed_flat, output_full), 'tensor', scat...  110 us
    all_gather x1, waiting for transfers between devices, local(): normed_two = lax.all_gather(normed_rows_two, 'tensor', axis=0, tiled=True)  65.5 us
    reduce_scatter x1, waiting for transfers between devices, local(): lax.psum_scatter((multiply_by_transpose(grad_q, query_full) + multiply_by...  61.1 us
    reduce_scatter x1, waiting for transfers between devices, local(): lax.psum_scatter((multiply_by_transpose(grad_gate_rows, gate_full) + mult...  60.5 us
    all_gather x1, waiting for transfers between devices, local(): lax.all_gather(cotangent.astype(jnp.bfloat16), 'tensor', axis=0, tiled=True)  57.4 us
    dot_general x14, matrix products, product(): jnp.einsum(formula, left_side, right_side, preferred_element_type=jnp.flo...  43.7 us
    all_gather x1, waiting for transfers between devices, local(): lax.all_gather(grad_resid.astype(jnp.bfloat16), 'tensor', axis=0, tiled=T...  39.9 us
    dot_general x7, matrix products, transposed_times(): lax.dot_general(left_side, right_side, (((0,), (0,)), ((), ())), preferre...  39 us
  transfers between devices with their start and end apart: 20, of which 17 were waited for; matrix products, arithmetic and copies ran while one was open for 20% of the time, Pallas kernels for 0%

commit v1 on v0

--- a/solution.py
+++ b/solution.py
@@ -232,7 +232,14 @@
         matrix_multiply(mixed_flat, output_full), "tensor", scatter_dimension=0, tiled=True
     )
     unit_two, inverse_two, normed_rows_two = norm_forward(residual, gain_two)
-    normed_two = lax.all_gather(normed_rows_two, "tensor", axis=0, tiled=True)
+    ring = [normed_rows_two]
+    for hop in range(3):
+        ring.append(lax.ppermute(ring[-1], "tensor", [(dev, (dev + 1) % 4) for dev in range(4)]))
+    normed_two = jnp.roll(
+        jnp.concatenate(ring[::-1], axis=0),
+        (lax.axis_index("tensor") + 1) * ring[0].shape[0],
+        axis=0,
+    )
     gate_rows = matrix_multiply(normed_two, gate_full)
     up_rows = matrix_multiply(normed_two, up_full)
     sigmoid_gate = jax.nn.sigmoid(gate_rows)

time: 1100 us -> 1060 us (0.964)
  waiting for transfers between devices: 749 us -> 677 us
  starting transfers between devices: 1.92 us -> 27.9 us
    all_gather x1 -> x0, waiting for transfers between devices: 65.5 us -> none  [local(): normed_two = lax.all_gather(normed_rows_two, 'tensor', axis=0, tiled=True)]
    ppermute x0 -> x3, waiting for transfers between devices: none -> 61.6 us  [local(): lax.ppermute(ring[-1], 'tensor', [(dev, (dev + 1) % 4) for dev in range(4)])]
    all_gather x1, waiting for transfers between devices: 57.4 us -> 0.83 us  [local(): lax.all_gather(cotangent.astype(jnp.bfloat16), 'tensor', axis=0, tiled=True)]
    ppermute x0 -> x3, starting transfers between devices: none -> 26.5 us  [local(): lax.ppermute(ring[-1], 'tensor', [(dev, (dev + 1) % 4) for dev in range(4)])]
    all_gather x1, waiting for transfers between devices: 27.5 us -> 15.7 us  [local(): lax.all_gather(w_up, 'dp', axis=0, tiled=True)]
  transfers between devices with their start and end apart: 20 -> 22, of which waited for: 17 -> 18; matrix products, arithmetic and copies ran while one was open for 20% -> 21% of each run, Pallas kernels for 0% -> 0%
where the time goes in v1:
time: 1060 us; the launch traced here: 1050 us
  waiting for transfers between devices  677 us (64%)
  matrix products  150 us (14%)
  local copies, waits for them, and re-layouts  67.3 us (6%)
  blocking collectives  61.4 us (6%)
  other arithmetic  49.3 us (5%)
  starting transfers between devices  27.9 us (3%)
  between operations  16.2 us (2%)
    reduce_scatter x1, waiting for transfers between devices, local(): lax.psum_scatter(matrix_multiply(mixed_flat, output_full), 'tensor', scat...  106 us
    ppermute x3, waiting for transfers between devices, local(): lax.ppermute(ring[-1], 'tensor', [(dev, (dev + 1) % 4) for dev in range(4)])  61.6 us
    reduce_scatter x1, waiting for transfers between devices, local(): lax.psum_scatter((multiply_by_transpose(grad_q, query_full) + multiply_by...  61 us
    reduce_scatter x1, waiting for transfers between devices, local(): lax.psum_scatter((multiply_by_transpose(grad_gate_rows, gate_full) + mult...  60.5 us
    dot_general x7, matrix products, matrix_multiply(): return jnp.dot(left_side, right_side, preferred_element_type=jnp.float32)  44.5 us
    dot_general x14, matrix products, product(): jnp.einsum(formula, left_side, right_side, preferred_element_type=jnp.flo...  39.9 us
    all_gather x1, waiting for transfers between devices, local(): lax.all_gather(grad_resid.astype(jnp.bfloat16), 'tensor', axis=0, tiled=T...  39.8 us
    all_gather x1, waiting for transfers between devices, local(): lax.all_gather(normed_rows_one, 'tensor', axis=0, tiled=True)  39.8 us
  transfers between devices with their start and end apart: 22, of which 18 were waited for; matrix products, arithmetic and copies ran while one was open for 21% of the time, Pallas kernels for 0%

profile of v1, /device:TPU:0, one launch (start us, length us, event | category | flops | bytes accessed | tf_op | source)
XLA Modules:
  0.0 1049.8 jit_solution(16941948533028186055)
XLA Ops:
  12.7 16.0 %all-reduce.6 = (bf16[1536]{0:T(1024)(128)(2,1)S(1)}, bf16[1536]{0:T(1024)(128)(2,1)}) all-reduce(bf16[1536]{0:T(1024)(128)(2,1)S(1)} %dynamic-update-slice, bf16[1536]{0:T(1024)(128)(2,1)S(1)} %dynamic-update-slice.1), channel_id=1, replica_groups=mesh['dp'=8,'tensor'=4] {'dp'}, use_global_device_ids=true, to_apply=%add | all-reduce | flops 3072 | bytes 12288
  54.4 39.8 %all-gather.9.cloned.1.call-done = bf16[1024,1536]{1,0:T(8,128)(2,1)} async-done(((bf16[256,1536]{1,0:T(8,128)(2,1)}), bf16[1024,1536]{1,0:T(8,128)(2,1)}) %all-gather.9.cloned.1.call-update) | async-done | bytes 3145744 | tf_op jit(solution)/shard_map/all_gather | solution.py:208
  97.4 21.3 %all-gather.11.cloned.1.call-done = bf16[1536,384]{1,0:T(8,128)(2,1)} async-done(((bf16[192,384]{1,0:T(8,128)(2,1)}), bf16[1536,384]{1,0:T(8,128)(2,1)}) %all-gather.11.cloned.1.call-update) | async-done | bytes 1179664 | tf_op jit(solution)/shard_map/all_gather | solution.py:185
  128.2 20.1 %while.27 = (s32[]{:T(128)}, bf16[2,512,2,2,96]{1,4,3,2,0:T(8,128)(2,1)}, f32[2,2,2,512]{3,2,1,0:T(2,128)}, s32[2,512]{1,0:T(2,128)}, s32[1024]{0:T(1024)S(1)}, ...) while((s32[]{:T(128)}, ...), condition=%wide.region_7.8_spmd, body=%wide.region_4.7_spmd.sunk | while | flops 830142464 | bytes 28917884 | solution.py:111
  161.2 106.5 %reduce-scatter.12.cloned.1.call-done = f32[256,1536]{1,0:T(8,128)} async-done(((f32[1024,1536]{1,0:T(8,128)}), f32[256,1536]{1,0:T(8,128)}) %reduce-scatter.12.cloned.1.call-update) | async-done | bytes 1572880 | tf_op jit(solution)/shard_map/reduce_scatter | solution.py:231
  271.7 29.2 %collective-permute-done = bf16[256,1536]{1,0:T(8,128)(2,1)S(1)} collective-permute-done((bf16[256,1536]{1,0:T(8,128)(2,1)S(1)}, bf16[256,1536]{1,0:T(8,128)(2,1)S(1)}, u32[]{:S(2)}, u32[]{:S(2)}) %collective-permute-start) | collective-permute-done | bytes 786464 | tf_op jit(solution)/shard_map/ppermute | solution.py:237
  312.7 32.4 %collective-permute-done.1 = bf16[256,1536]{1,0:T(8,128)(2,1)S(1)} collective-permute-done((bf16[256,1536]{1,0:T(8,128)(2,1)S(1)}, bf16[256,1536]{1,0:T(8,128)(2,1)S(1)}, u32[]{:S(2)}, u32[]{:S(2)}) %collective-permute-start.1) | collective-permute-done | bytes 786464 | tf_op jit(solution)/shard_map/ppermute | solution.py:237
  345.1 13.2 %collective-permute-start.2 = (bf16[256,1536]{1,0:T(8,128)(2,1)S(1)}, bf16[256,1536]{1,0:T(8,128)(2,1)}, u32[]{:S(2)}, u32[]{:S(2)}) collective-permute-start(bf16[256,1536]{1,0:T(8,128)(2,1)S(1)} %collective-permute-done.1), channel_id=1, source_target_pairs={{0,1},{1,2},{2,3},{3,0},{4,5},{5,6},{6,7},{7,4},{8,9},{9,10},{10,1... | collective-permute-start | bytes 2359304 | tf_op jit(solution)/shard_map/ppermute | solution.py:237
  359.2 32.2 %all-gather.19.cloned.1.call-done = bf16[1024,1536]{0,1:T(8,128)(2,1)} async-done(((bf16[1024,192]{0,1:T(8,128)(2,1)}), bf16[1024,1536]{0,1:T(8,128)(2,1)}) %all-gather.19.cloned.1.call-update) | async-done | bytes 3145744 | tf_op jit(solution)/shard_map/all_gather | solution.py:191
  409.8 15.7 %all-gather.17.cloned.1.call-done = bf16[1536,1024]{1,0:T(8,128)(2,1)} async-done(((bf16[192,1024]{1,0:T(8,128)(2,1)}), bf16[1536,1024]{1,0:T(8,128)(2,1)}) %all-gather.17.cloned.1.call-update) | async-done | bytes 3145744 | tf_op jit(solution)/shard_map/all_gather | solution.py:190
  433.6 25.9 %all-gather.15.cloned.1.call-done = bf16[1536,1024]{1,0:T(8,128)(2,1)} async-done(((bf16[192,1024]{1,0:T(8,128)(2,1)}), bf16[1536,1024]{1,0:T(8,128)(2,1)}) %all-gather.15.cloned.1.call-update) | async-done | bytes 3145744 | tf_op jit(solution)/shard_map/all_gather | solution.py:189
  480.0 60.5 %reduce-scatter.16.cloned.1.call-done = bf16[256,1536]{1,0:T(8,128)(2,1)} async-done(((bf16[1024,1536]{1,0:T(8,128)(2,1)}), bf16[256,1536]{1,0:T(8,128)(2,1)}) %reduce-scatter.16.cloned.1.call-update) | async-done | bytes 786448 | tf_op jit(solution)/shard_map/reduce_scatter | solution.py:292
  569.5 39.8 %all-gather.23.cloned.1.call-done = bf16[1024,1536]{1,0:T(8,128)(2,1)} async-done(((bf16[256,1536]{1,0:T(8,128)(2,1)}), bf16[1024,1536]{1,0:T(8,128)(2,1)}) %all-gather.23.cloned.1.call-update) | async-done | bytes 3145744 | tf_op jit(solution)/shard_map/all_gather | solution.py:303
  622.2 66.8 %while.28 = (s32[]{:T(128)}, f32[1024,2,96]{0,2,1:T(8,128)}, f32[1024,2,96]{0,2,1:T(8,128)}, f32[2,512,2,2,96]{1,0,4,3,2:T(2,128)}, bf16[2,512,2,2,96]{1,4,3,2,0...) while((s32[]{:T(128)}, f32[1024,2,96]{0,2,1:T(8,128)}, ...), condition=%wide.region_15.16_spmd.clone, body=%wide.region_13.15_spmd.clone.sunk | while | flops 2039478272 | bytes 50004156 | solution.py:150
  639.8 15.0 %dynamic_update_slice.20 = f32[2,512,2,2,96]{1,0,4,3,2:T(2,128)} dynamic-update-slice(f32[2,512,2,2,96]{1,0,4,3,2:T(2,128)} %get-tuple-element.535, f32[1,512,2,2,96]{1,0,4,3,2:T(1,128)S(1)} %copy.60, s32[]{:T(128)S(6)} %copy.86, s32[]{:T(128)} %constant.85.clone.1..sunk, s32[]{:T(128)} %constant.85.clone.1..sunk, s32[]{:T(128)} %constant.85.clone.1..sunk, s32[]{:T(128)} %constant.85.clone.1..sunk) | dynamic-update-slice | bytes 1572868 | tf_op jit(solution)/shard_map/while/body/jit(dynamic_update_index_in_dim)/dynamic_update_slice | solution.py:150
  673.9 15.1 %dynamic_update_slice.20 = f32[2,512,2,2,96]{1,0,4,3,2:T(2,128)} dynamic-update-slice(f32[2,512,2,2,96]{1,0,4,3,2:T(2,128)} %get-tuple-element.535, f32[1,512,2,2,96]{1,0,4,3,2:T(1,128)S(1)} %copy.60, s32[]{:T(128)S(6)} %copy.86, s32[]{:T(128)} %constant.85.clone.1..sunk, s32[]{:T(128)} %constant.85.clone.1..sunk, s32[]{:T(128)} %constant.85.clone.1..sunk, s32[]{:T(128)} %constant.85.clone.1..sunk) | dynamic-update-slice | bytes 1572868 | tf_op jit(solution)/shard_map/while/body/jit(dynamic_update_index_in_dim)/dynamic_update_slice | solution.py:150
  732.7 23.6 %reduce-scatter.28.cloned.1.call-done = bf16[192,1024]{1,0:T(8,128)(2,1)} async-done(((bf16[1536,1024]{1,0:T(8,128)(2,1)}), bf16[192,1024]{1,0:T(8,128)(2,1)}) %reduce-scatter.28.cloned.1.call-update) | async-done | bytes 393232 | tf_op jit(solution)/shard_map/reduce_scatter | solution.py:350
  758.3 36.0 %reduce-scatter.24.cloned.1.call-done = bf16[192,192]{1,0:T(8,128)(2,1)} async-done(((bf16[1536,192]{1,0:T(8,128)(2,1)}), bf16[192,192]{1,0:T(8,128)(2,1)}) %reduce-scatter.24.cloned.1.call-update) | async-done | bytes 73744 | tf_op jit(solution)/shard_map/reduce_scatter | solution.py:344
  795.9 36.4 %reduce-scatter.22.cloned.1.call-done = bf16[192,192]{1,0:T(8,128)(2,1)} async-done(((bf16[1536,192]{1,0:T(8,128)(2,1)}), bf16[192,192]{1,0:T(8,128)(2,1)}) %reduce-scatter.22.cloned.1.call-update) | async-done | bytes 73744 | tf_op jit(solution)/shard_map/reduce_scatter | solution.py:341
  833.9 38.8 %reduce-scatter.26.cloned.1.call-done = bf16[384,192]{0,1:T(8,128)(2,1)} async-done(((bf16[384,1536]{0,1:T(8,128)(2,1)}), bf16[384,192]{0,1:T(8,128)(2,1)}) %reduce-scatter.26.cloned.1.call-update) | async-done | bytes 147472 | tf_op jit(solution)/shard_map/reduce_scatter | solution.py:347
  874.3 38.7 %reduce-scatter.20.cloned.1.call-done = bf16[192,384]{1,0:T(8,128)(2,1)} async-done(((bf16[1536,384]{1,0:T(8,128)(2,1)}), bf16[192,384]{1,0:T(8,128)(2,1)}) %reduce-scatter.20.cloned.1.call-update) | async-done | bytes 147472 | tf_op jit(solution)/shard_map/reduce_scatter | solution.py:338
  914.7 61.0 %reduce-scatter.18.cloned.1.call-done = bf16[256,1536]{1,0:T(8,128)(2,1)} async-done(((bf16[1024,1536]{1,0:T(8,128)(2,1)}), bf16[256,1536]{1,0:T(8,128)(2,1)}) %reduce-scatter.18.cloned.1.call-update) | async-done | bytes 786448 | tf_op jit(solution)/shard_map/reduce_scatter | solution.py:325
  977.4 13.5 %all-reduce.5 = (bf16[1536]{0:T(1024)(128)(2,1)S(1)}, bf16[1536]{0:T(1024)(128)(2,1)S(1)}) all-reduce(bf16[1536]{0:T(1024)(128)(2,1)S(1)} %get-tuple-element.256, bf16[1536]{0:T(1024)(128)(2,1)S(1)} %copy-done.32), channel_id=13, replica_groups=mesh['dp'=8,'tensor'=4] {'dp'}, use_global_device_ids=true, to_apply=%region_26.27.clone | all-reduce | flops 3072 | bytes 12288
  1003.0 35.5 %reduce-scatter.14.cloned.1.call-done = bf16[256,1536]{1,0:T(8,128)(2,1)} async-done(((bf16[1024,1536]{1,0:T(8,128)(2,1)}), bf16[256,1536]{1,0:T(8,128)(2,1)}) %reduce-scatter.14.cloned.1.call-update) | async-done | bytes 786448 | tf_op jit(solution)/shard_map/reduce_scatter | solution.py:255
  (248 shorter events, 287.0 us)
Async XLA Ops:
  7.2 87.0 %all-gather.9.cloned.1.call-start = ((), (), s32[]{:S(2)}) async-start(), calls=%async_computation.11 | async-start | bytes 3932160 | tf_op jit(solution)/shard_map/all_gather | solution.py:208
  31.2 87.4 %all-gather.11.cloned.1.call-start = ((), (), s32[]{:S(2)}) async-start(), calls=%async_computation.12 | async-start | bytes 1327104 | tf_op jit(solution)/shard_map/all_gather | solution.py:185
  32.0 118.7 %all-gather.13.cloned.1.call-start = ((), (), s32[]{:S(2)}) async-start(), calls=%async_computation.13 | async-start | bytes 1327104 | tf_op jit(solution)/shard_map/all_gather | solution.py:188
  32.7 234.9 %reduce-scatter.12.cloned.1.call-start = ((), (), s32[]{:S(2)}) async-start(), calls=%async_computation.14 | async-start | bytes 7864320 | tf_op jit(solution)/shard_map/reduce_scatter | solution.py:231
  156.8 202.4 %all-gather.21.cloned.1.call-start = ((), (), s32[]{:S(2)}) async-start(), calls=%async_computation.19 | async-start | bytes 3932160 | tf_op jit(solution)/shard_map/all_gather | solution.py:283
  159.1 232.2 %all-gather.19.cloned.1.call-start = ((), (), s32[]{:S(2)}) async-start(), calls=%async_computation.17 | async-start | bytes 3538944 | tf_op jit(solution)/shard_map/all_gather | solution.py:191
  159.7 265.8 %all-gather.17.cloned.1.call-start = ((), (), s32[]{:S(2)}) async-start(), calls=%async_computation.16 | async-start | bytes 3538944 | tf_op jit(solution)/shard_map/all_gather | solution.py:190
  160.4 299.1 %all-gather.15.cloned.1.call-start = ((), (), s32[]{:S(2)}) async-start(), calls=%async_computation.15 | async-start | bytes 3538944 | tf_op jit(solution)/shard_map/all_gather | solution.py:189
  270.1 30.8 %collective-permute-start = (bf16[256,1536]{1,0:T(8,128)(2,1)S(1)}, bf16[256,1536]{1,0:T(8,128)(2,1)S(1)}, u32[]{:S(2)}, u32[]{:S(2)}) collective-permute-start(bf16[256,1536]{1,0:T(8,128)(2,1)S(1)} %multiply_convert_fusion.3), channel_id=1, source_target_pairs={{0,1},{1,2},{2,3},{3,0},{4,5},{5,6},{6,7},{7,4},{8,9},{9,10},{10,1... | collective-permute-start | bytes 2359304 | tf_op jit(solution)/shard_map/ppermute | solution.py:237
  271.7 268.8 %reduce-scatter.16.cloned.1.call-start = ((), (), s32[]{:S(2)}) async-start(), calls=%async_computation.20 | async-start | bytes 3932160 | tf_op jit(solution)/shard_map/reduce_scatter | solution.py:292
  300.9 44.2 %collective-permute-start.1 = (bf16[256,1536]{1,0:T(8,128)(2,1)S(1)}, bf16[256,1536]{1,0:T(8,128)(2,1)S(1)}, u32[]{:S(2)}, u32[]{:S(2)}) collective-permute-start(bf16[256,1536]{1,0:T(8,128)(2,1)S(1)} %collective-permute-done), channel_id=1, source_target_pairs={{0,1},{1,2},{2,3},{3,0},{4,5},{5,6},{6,7},{7,4},{8,9},{9,10},{10,1... | collective-permute-start | bytes 2359304 | tf_op jit(solution)/shard_map/ppermute | solution.py:237
  345.1 54.5 %collective-permute-start.2 = (bf16[256,1536]{1,0:T(8,128)(2,1)S(1)}, bf16[256,1536]{1,0:T(8,128)(2,1)}, u32[]{:S(2)}, u32[]{:S(2)}) collective-permute-start(bf16[256,1536]{1,0:T(8,128)(2,1)S(1)} %collective-permute-done.1), channel_id=1, source_target_pairs={{0,1},{1,2},{2,3},{3,0},{4,5},{5,6},{6,7},{7,4},{8,9},{9,10},{10,1... | collective-permute-start | bytes 2359304 | tf_op jit(solution)/shard_map/ppermute | solution.py:237
  480.0 129.4 %all-gather.23.cloned.1.call-start = ((), (), s32[]{:S(2)}) async-start(), calls=%async_computation.21 | async-start | bytes 3932160 | tf_op jit(solution)/shard_map/all_gather | solution.py:303
  545.9 182.9 %reduce-scatter.32.cloned.1.call-start = ((), (), s32[]{:S(2)}) async-start(), calls=%async_computation.29 | async-start | bytes 3538944 | tf_op jit(solution)/shard_map/reduce_scatter | solution.py:356
  553.7 177.1 %reduce-scatter.30.cloned.1.call-start = ((), (), s32[]{:S(2)}) async-start(), calls=%async_computation.28 | async-start | bytes 3538944 | tf_op jit(solution)/shard_map/reduce_scatter | solution.py:353
  561.7 194.6 %reduce-scatter.28.cloned.1.call-start = ((), (), s32[]{:S(2)}) async-start(), calls=%async_computation.27 | async-start | bytes 3538944 | tf_op jit(solution)/shard_map/reduce_scatter | solution.py:350
  569.5 224.8 %reduce-scatter.24.cloned.1.call-start = ((), (), s32[]{:S(2)}) async-start(), calls=%async_computation.25 | async-start | bytes 884736 | tf_op jit(solution)/shard_map/reduce_scatter | solution.py:344
  694.9 137.4 %reduce-scatter.22.cloned.1.call-start = ((), (), s32[]{:S(2)}) async-start(), calls=%async_computation.24 | async-start | bytes 884736 | tf_op jit(solution)/shard_map/reduce_scatter | solution.py:341
  701.3 171.4 %reduce-scatter.26.cloned.1.call-start = ((), (), s32[]{:S(2)}) async-start(), calls=%async_computation.26 | async-start | bytes 1327104 | tf_op jit(solution)/shard_map/reduce_scatter | solution.py:347
  706.1 206.9 %reduce-scatter.20.cloned.1.call-start = ((), (), s32[]{:S(2)}) async-start(), calls=%async_computation.23 | async-start | bytes 1327104 | tf_op jit(solution)/shard_map/reduce_scatter | solution.py:338
  713.6 262.1 %reduce-scatter.18.cloned.1.call-start = ((), (), s32[]{:S(2)}) async-start(), calls=%async_computation.22 | async-start | bytes 3932160 | tf_op jit(solution)/shard_map/reduce_scatter | solution.py:325
  719.7 318.9 %reduce-scatter.14.cloned.1.call-start = ((), (), s32[]{:S(2)}) async-start(), calls=%async_computation.18 | async-start | bytes 3932160 | tf_op jit(solution)/shard_map/reduce_scatter | solution.py:255
  730.7 307.8 %copy-start.29 = (f32[256]{0:T(256)S(1)}, f32[256]{0:T(256)}, u32[]{:S(2)}) copy-start(f32[256]{0:T(256)} %copy-done.27) | copy-start | bytes 3076
  730.7 307.8 %copy-start.34 = (f32[256]{0:T(256)S(1)}, f32[256]{0:T(256)}, u32[]{:S(2)}) copy-start(f32[256]{0:T(256)} %copy-done.33) | copy-start | bytes 3076
  (38 other events, 1671.3 us)
Sparse Core Ops, SparseCore 0:
  31.4 62.7 all-gather.8
  96.1 22.5 all-gather.10
  120.6 23.9 all-gather.12
  156.9 110.7 reduce-scatter.11
  269.7 89.4 all-gather.20
  360.9 30.3 all-gather.18
  393.2 32.1 all-gather.16
  427.3 32.1 all-gather.14
  480.1 60.3 reduce-scatter.15
  546.0 63.3 all-gather.22
  612.8 44.6 reduce-scatter.31
  660.7 46.0 reduce-scatter.29
  710.2 46.0 reduce-scatter.27
  759.3 34.9 reduce-scatter.23
  797.3 34.9 reduce-scatter.21
  836.0 36.6 reduce-scatter.25
  876.3 36.6 reduce-scatter.19
  915.2 60.4 reduce-scatter.17
  978.0 60.5 reduce-scatter.13
